TPU v7x, 128 devices: a whole 4x4x4 slice. The times are simulated.
128 devices in a mesh: lat: 4 (over z_hi, core), lon: 32 (over y, z_lo, x).
Axes of the slice: x: 4, y: 4, z: 4 (z_hi: 2, z_lo: 2; z = z_hi * 2 + z_lo), core: 2. Of those that a mesh axis runs over, the one named last changes fastest.
Arguments:
- features: bfloat16 [8, 128, 1024, 256], P(None, 'lat', 'lon'), may hold values from -16 to 16
- band_points: int32 [128], replicated, may hold values from 256 to 1024, as said below
- survival_flags: int32 [8, 2], replicated, may hold values 0 or 1
- first_kernel_weight: bfloat16 [3, 3, 256, 256], replicated, may hold values from -0.125 to 0.125
- second_kernel_weight: bfloat16 [3, 3, 256, 256], replicated, may hold values from -0.125 to 0.125
Outputs:
- section_result: bfloat16 [8, 128, 1024, 256], P(None, 'lat', 'lon')
Inputs may be any that keep to these rules, and one draw needn't show every extreme that they name: `band_points`: the live points of a row are its first ones.
All inputs are finite; a program needn't handle non-finite values.
Results may differ from a plain program's by a relative error of at most 0.0006.
The roundings to bfloat16 on the way count: a program that leaves them out, or rounds other values in their place, can miss the bound.
Values may be sent and summed in bfloat16 or wider, within the bound.
No kernel may reach another device: no remote copies, remote signals or barrier semaphores. Data moves between devices by JAX's collectives and lax.ppermute only.
A program may use at most 320 MiB of HBM per device.

v0:
```python
import jax
import jax.numpy as jnp
from jax import lax
from jax.sharding import PartitionSpec as P

GROUPS = 32
FIRST_DILATION = 2
SECOND_DILATION = 4
EPS = 1e-05
KEEP_RATE = 0.8


def extended(array, sides, width, wrap):
    for axis, dim in sides:
        peers, length = (lax.axis_size(axis), array.shape[dim])
        up = [(i, (i + 1) % peers) for i in range(peers if wrap else peers - 1)]
        down = [(j, i) for i, j in up]
        last = lax.slice_in_dim(array, length - width, length, axis=dim)
        leading = lax.slice_in_dim(array, 0, width, axis=dim)
        before = lax.ppermute(last, axis, up)
        after = lax.ppermute(leading, axis, down)
        array = jnp.concatenate([before, array, after], axis=dim)
    return array


def widen_border(field_in, reach_cells):
    lat_padded = extended(field_in, (("lat", 1),), reach_cells, False)
    return extended(lat_padded, (("lon", 2),), reach_cells, True)


def live_cells(band_points, tile_rows, tile_cols, margin):
    lat_total = band_points.shape[0]
    lon_total = tile_cols * lax.axis_size("lon")
    row_index = (
        lax.axis_index("lat") * tile_rows
        - margin
        + jnp.arange(tile_rows + 2 * margin, dtype=jnp.int32)
    )
    col_index = (
        lax.axis_index("lon") * tile_cols
        - margin
        + jnp.arange(tile_cols + 2 * margin, dtype=jnp.int32)
    )
    col_index = jnp.mod(col_index, lon_total)
    matches = row_index[:, None] == jnp.arange(lat_total, dtype=jnp.int32)[None, :]
    row_points = jnp.sum(jnp.where(matches, band_points[None, :], 0), axis=1)
    return (col_index[None, :] < row_points[:, None]).astype(jnp.float32)


def statistics(values_in, live_mask, live_count, group_size):
    samples = values_in.shape[0]
    masked = values_in * live_mask[None, :, :, None]

    def group_total(chan_sums):
        return chan_sums.reshape(samples, GROUPS, group_size).sum(axis=2)

    group_means = lax.psum(group_total(jnp.sum(masked, axis=(1, 2))), ("lat", "lon")) / live_count
    shifted = values_in - jnp.repeat(group_means, group_size, axis=1)[:, None, None, :]
    squares = shifted * shifted * live_mask[None, :, :, None]
    group_vars = lax.psum(group_total(jnp.sum(squares, axis=(1, 2))), ("lat", "lon")) / live_count
    return (group_means, group_vars)


def activate(values_in, group_means, group_vars, live_mask, group_size):
    centre = jnp.repeat(group_means, group_size, axis=1)[:, None, None, :]
    inv_std = jnp.repeat(lax.rsqrt(group_vars + EPS), group_size, axis=1)[:, None, None, :]
    return (jax.nn.silu((values_in - centre) * inv_std) * live_mask[None, :, :, None]).astype(
        jnp.bfloat16
    )


def apply_kernel(padded, weight, dilation):
    out_rows = padded.shape[1] - 2 * dilation
    out_cols = padded.shape[2] - 2 * dilation
    summed = None
    for row_tap in range(3):
        for col_tap in range(3):
            shifted = padded[
                :,
                row_tap * dilation : row_tap * dilation + out_rows,
                col_tap * dilation : col_tap * dilation + out_cols,
                :,
            ]
            tap_term = jnp.einsum(
                "bijc,cd->bijd",
                shifted,
                weight[row_tap, col_tap],
                preferred_element_type=jnp.float32,
            )
            summed = tap_term if summed is None else summed + tap_term
    return summed


def residual_branch(padded, weight, dilation, kept):
    result = apply_kernel(padded, weight, dilation)
    return result * (kept.astype(jnp.float32) / KEEP_RATE)[:, None, None, None]


def per_device(features, band_points, survival_flags, first_kernel_weight, second_kernel_weight):
    tile_rows = features.shape[1]
    tile_cols = features.shape[2]
    group_size = features.shape[3] // GROUPS
    live_count = jnp.sum(band_points).astype(jnp.float32) * group_size
    live_inner = live_cells(band_points, tile_rows, tile_cols, 0)
    initial_feature_map = features.astype(jnp.float32)
    first_means, first_vars = statistics(initial_feature_map, live_inner, live_count, group_size)
    first_hidden = activate(initial_feature_map, first_means, first_vars, live_inner, group_size)
    first_result = (
        initial_feature_map
        + residual_branch(
            widen_border(first_hidden, FIRST_DILATION),
            first_kernel_weight,
            FIRST_DILATION,
            survival_flags[:, 0],
        )
    ).astype(jnp.bfloat16)
    first_result = lax.optimization_barrier(first_result)
    first_feature_map = first_result.astype(jnp.float32)
    second_means, second_vars = statistics(first_feature_map, live_inner, live_count, group_size)
    second_hidden = activate(first_feature_map, second_means, second_vars, live_inner, group_size)
    section_result = first_feature_map + residual_branch(
        widen_border(second_hidden, SECOND_DILATION),
        second_kernel_weight,
        SECOND_DILATION,
        survival_flags[:, 1],
    )
    return section_result.astype(jnp.bfloat16)


def solution(mesh):
    in_specs = (P(None, "lat", "lon", None), P(), P(), P(), P())
    out_specs = P(None, "lat", "lon", None)
    return jax.shard_map(
        per_device, mesh=mesh, in_specs=in_specs, out_specs=out_specs, check_vma=False
    )
```

profile of v0, /device:TPU:1, one launch (start us, length us, event | category | flops | bytes accessed | tf_op | source)
XLA Modules:
  0.0 468.8 jit_solution(17577725118338050617)
XLA Ops:
  4.2 68.7 %psum.28 = f32[8,32]{1,0:T(8,128)S(1)} all-reduce(f32[8,32]{1,0:T(8,128)S(1)} %reduce_sum.92), channel_id=1, replica_groups=mesh['lat'=4,'lon'=32] {'lat','lon'}, use_global_device_ids=true, to_apply=%region_3.4 | all-reduce | flops 256 | bytes 2048 | tf_op jit(solution)/shard_map/psum | solution.py:57
  75.1 3.7 fusion.21
  79.0 62.6 %psum.29 = f32[8,32]{1,0:T(8,128)S(1)} all-reduce(f32[8,32]{1,0:T(8,128)S(1)} %reduce_sum.95), channel_id=1, replica_groups=mesh['lat'=4,'lon'=32] {'lat','lon'}, use_global_device_ids=true, to_apply=%region_7.8 | all-reduce | flops 256 | bytes 2048 | tf_op jit(solution)/shard_map/psum | solution.py:60
  141.9 4.3 fusion.12
  146.2 3.8 collective-permute-start
  152.0 4.5 fusion.84
  160.8 5.2 %collective-permute-start.3 = (bf16[8,36,2,256]{3,2,1,0:T(2,128)(2,1)S(1)}, bf16[8,36,2,256]{3,2,1,0:T(2,128)(2,1)S(1)}, u32[]{:S(2)}, u32[]{:S(2)}) collective-permute-start(bf16[8,36,2,256]{3,2,1,0:T(2,128)(2,1)S(1)} %get-tuple-element.11), channel_id=1, source_target_pairs={{1,0},{2,1},{3,2},{4,3},{5,4},{6,5},{7,6},{8,7},{9,8},{10,9},{11,1... | collective-permute-start | bytes 884744 | tf_op jit(solution)/shard_map/ppermute | solution.py:21
  165.9 4.5 fusion.34
  170.4 4.5 fusion.38
  174.9 7.4 %pad_maximum_fusion.1 = (bf16[8,36,34,256]{3,2,1,0:T(8,128)(2,1)S(1)}, bf16[8,36,34,256]{3,2,1,0:T(8,128)(2,1)S(1)}) fusion(bf16[8,36,2,256]{3,2,1,0:T(2,128)(2,1)S(1)} %collective-permute-done.3, bf16[8,2,32,256]{3,2,1,0:T(8,128)(2,1)S(1)} %collective-permute-done.1, bf16[8,32,32,256]{3,2,1,0:T(8,128)(2,1)S(1)} %fusion.12, ...), kind=kLoop, calls=%fused_computation.35 | loop fusion | flops 40108032 | bytes 15335424 | tf_op jit(solution)/shard_map/concatenate | solution.py:22
  182.3 4.9 %fusion.56 = f32[8,32,32,256]{3,2,1,0:T(8,128)} fusion(bf16[8,36,34,256]{3,2,1,0:T(8,128)(2,1)S(1)} %get-tuple-element.10, bf16[3,3,256,256]{3,2,1,0:T(8,128)(2,1)S(1)} %copy-done.2), kind=kOutput, calls=%fused_computation.66 | convolution fusion | flops 1073741824 | bytes 12713984 | tf_op jit(solution)/shard_map/bijc,cd->bijd/dot_general | solution.py:84
  187.2 4.4 fusion.60
  191.6 4.5 fusion.58
  196.1 4.5 fusion.62
  200.6 4.5 fusion.64
  205.1 26.7 %fusion.23 = bf16[8,32,32,256]{3,2,1,0:T(8,128)(2,1)} fusion(bf16[8,32,32,256]{3,2,1,0:T(8,128)(2,1)} %param.5, f32[8,32,32,256]{3,2,1,0:T(8,128)} %fusion.38, f32[8,32,32,256]{3,2,1,0:T(8,128)} %fusion.56, f32[8,32,32,256]{3,2,1,0:T(8,128)} %fusion.58, f32[8,32,32,256]{3,2,1,0:T(8,128)} %fusion.84, f32[8,32,32,256]{3,2,1,0:T(8,128)} %fusion.60, ...), kind=kOutput, calls=%fused_computation.29 | convolution fusion | flops 1098907648 | bytes 79823360 | tf_op jit(solution)/shard_map/bijc,cd->bijd/dot_general | solution.py:84
  235.1 62.3 %psum.30 = f32[8,32]{1,0:T(8,128)S(1)} all-reduce(f32[8,32]{1,0:T(8,128)S(1)} %reduce_sum.97), channel_id=1, replica_groups=mesh['lat'=4,'lon'=32] {'lat','lon'}, use_global_device_ids=true, to_apply=%region_10.11 | all-reduce | flops 256 | bytes 2048 | tf_op jit(solution)/shard_map/psum | solution.py:57
  301.5 62.9 %psum.31 = f32[8,32]{1,0:T(8,128)S(1)} all-reduce(f32[8,32]{1,0:T(8,128)S(1)} %reduce_sum.99), channel_id=1, replica_groups=mesh['lat'=4,'lon'=32] {'lat','lon'}, use_global_device_ids=true, to_apply=%region_13.14 | all-reduce | flops 256 | bytes 2048 | tf_op jit(solution)/shard_map/psum | solution.py:60
  364.6 4.3 fusion.17
  369.0 4.1 collective-permute-start.4
  375.0 4.5 fusion.74
  379.5 19.6 %collective-permute-done.5 = bf16[8,4,32,256]{3,2,1,0:T(8,128)(2,1)S(1)} collective-permute-done((bf16[8,4,32,256]{3,2,1,0:T(8,128)(2,1)S(1)}, bf16[8,4,32,256]{3,2,1,0:T(8,128)(2,1)S(1)}, u32[]{:S(2)}, u32[]{:S(2)}) %collective-permute-start.5) | collective-permute-done | bytes 524320 | tf_op jit(solution)/shard_map/ppermute | solution.py:21
  399.8 5.9 %collective-permute-start.7 = (bf16[8,40,4,256]{3,2,1,0:T(4,128)(2,1)S(1)}, bf16[8,40,4,256]{3,2,1,0:T(4,128)(2,1)S(1)}, u32[]{:S(2)}, u32[]{:S(2)}) collective-permute-start(bf16[8,40,4,256]{3,2,1,0:T(4,128)(2,1)S(1)} %get-tuple-element.7), channel_id=1, source_target_pairs={{1,0},{2,1},{3,2},{4,3},{5,4},{6,5},{7,6},{8,7},{9,8},{10,9},{11,1... | collective-permute-start | bytes 1966088 | tf_op jit(solution)/shard_map/ppermute | solution.py:21
  405.7 4.4 fusion.26
  410.1 4.5 fusion.30
  414.6 4.5 pad_maximum_fusion
  419.1 4.9 %fusion.44 = f32[8,32,32,256]{3,2,1,0:T(8,128)} fusion(bf16[8,40,36,256]{3,2,1,0:T(8,128)(2,1)S(1)} %get-tuple-element.6, bf16[3,3,256,256]{3,2,1,0:T(8,128)(2,1)S(1)} %copy-done.3), kind=kOutput, calls=%fused_computation.54 | convolution fusion | flops 1073741824 | bytes 12713984 | tf_op jit(solution)/shard_map/bijc,cd->bijd/dot_general | solution.py:84
  424.0 4.5 fusion.48
  428.4 4.5 fusion.46
  432.9 4.5 fusion.50
  437.4 4.5 fusion.52
  441.9 26.7 %fusion.25 = bf16[8,32,32,256]{3,2,1,0:T(8,128)(2,1)} fusion(bf16[8,32,32,256]{3,2,1,0:T(8,128)(2,1)} %fusion.23, f32[8,32,32,256]{3,2,1,0:T(8,128)} %fusion.30, f32[8,32,32,256]{3,2,1,0:T(8,128)} %fusion.44, f32[8,32,32,256]{3,2,1,0:T(8,128)} %fusion.46, f32[8,32,32,256]{3,2,1,0:T(8,128)} %fusion.74, f32[8,32,32,256]{3,2,1,0:T(8,128)} %fusion.48, ...), kind=kOutput, calls=%fused_computation.31 | convolution fusion | flops 1098907648 | bytes 79823360 | tf_op jit(solution)/shard_map/bijc,cd->bijd/dot_general | solution.py:84
  (54 shorter events, 22.6 us)
Async XLA Ops:
  75.1 76.9 %copy-start.2 = (bf16[3,3,256,256]{3,2,1,0:T(8,128)(2,1)S(1)}, bf16[3,3,256,256]{3,2,1,0:T(8,128)(2,1)}, u32[]{:S(2)}) copy-start(bf16[3,3,256,256]{3,2,1,0:T(8,128)(2,1)} %param.8) | copy-start | bytes 3538948
  146.2 10.3 %collective-permute-start = (bf16[8,2,32,256]{3,2,1,0:T(8,128)(2,1)S(1)}, bf16[8,2,32,256]{3,2,1,0:T(8,128)(2,1)S(1)}, u32[]{:S(2)}, u32[]{:S(2)}) collective-permute-start(bf16[8,2,32,256]{3,2,1,0:T(8,128)(2,1)S(1)} %get-tuple-element.15), channel_id=1, source_target_pairs={{0,32},{32,64},{64,96},{1,33},{33,65},{65,97},{2,34},{34,66},{66,9... | collective-permute-start | bytes 786440 | tf_op jit(solution)/shard_map/ppermute | solution.py:20
  150.1 6.4 %copy-start.4 = (s32[8,2]{0,1:T(2,128)S(1)}, s32[8,2]{0,1:T(2,128)}, u32[]{:S(2)}) copy-start(s32[8,2]{0,1:T(2,128)} %param.7) | copy-start | bytes 196
  150.1 9.2 %collective-permute-start.1 = (bf16[8,2,32,256]{3,2,1,0:T(8,128)(2,1)S(1)}, bf16[8,2,32,256]{3,2,1,0:T(8,128)(2,1)S(1)}, u32[]{:S(2)}, u32[]{:S(2)}) collective-permute-start(bf16[8,2,32,256]{3,2,1,0:T(8,128)(2,1)S(1)} %get-tuple-element.16), channel_id=1, source_target_pairs={{32,0},{64,32},{96,64},{33,1},{65,33},{97,65},{34,2},{66,34},{98,6... | collective-permute-start | bytes 786440 | tf_op jit(solution)/shard_map/ppermute | solution.py:21
  159.7 15.1 %collective-permute-start.2 = (bf16[8,36,2,256]{3,2,1,0:T(2,128)(2,1)S(1)}, bf16[8,36,2,256]{3,2,1,0:T(2,128)(2,1)S(1)}, u32[]{:S(2)}, u32[]{:S(2)}) collective-permute-start(bf16[8,36,2,256]{3,2,1,0:T(2,128)(2,1)S(1)} %get-tuple-element.12), channel_id=1, source_target_pairs={{0,1},{1,2},{2,3},{3,4},{4,5},{5,6},{6,7},{7,8},{8,9},{9,10},{10,1... | collective-permute-start | bytes 884744 | tf_op jit(solution)/shard_map/ppermute | solution.py:20
  160.8 14.1 %collective-permute-start.3 = (bf16[8,36,2,256]{3,2,1,0:T(2,128)(2,1)S(1)}, bf16[8,36,2,256]{3,2,1,0:T(2,128)(2,1)S(1)}, u32[]{:S(2)}, u32[]{:S(2)}) collective-permute-start(bf16[8,36,2,256]{3,2,1,0:T(2,128)(2,1)S(1)} %get-tuple-element.11), channel_id=1, source_target_pairs={{1,0},{2,1},{3,2},{4,3},{5,4},{6,5},{7,6},{8,7},{9,8},{10,9},{11,1... | collective-permute-start | bytes 884744 | tf_op jit(solution)/shard_map/ppermute | solution.py:21
  182.3 13.8 %copy-start = (bf16[8,36,34,256]{3,2,1,0:T(8,128)(2,1)}, bf16[8,36,34,256]{3,2,1,0:T(8,128)(2,1)S(1)}, u32[]{:S(2)}) copy-start(bf16[8,36,34,256]{3,2,1,0:T(8,128)(2,1)S(1)} %get-tuple-element.9) | copy-start | bytes 15040516
  301.2 73.8 %copy-start.3 = (bf16[3,3,256,256]{3,2,1,0:T(8,128)(2,1)S(1)}, bf16[3,3,256,256]{3,2,1,0:T(8,128)(2,1)}, u32[]{:S(2)}) copy-start(bf16[3,3,256,256]{3,2,1,0:T(8,128)(2,1)} %param.9) | copy-start | bytes 3538948
  369.0 10.5 %collective-permute-start.4 = (bf16[8,4,32,256]{3,2,1,0:T(8,128)(2,1)S(1)}, bf16[8,4,32,256]{3,2,1,0:T(8,128)(2,1)S(1)}, u32[]{:S(2)}, u32[]{:S(2)}) collective-permute-start(bf16[8,4,32,256]{3,2,1,0:T(8,128)(2,1)S(1)} %get-tuple-element.13), channel_id=1, source_target_pairs={{0,32},{32,64},{64,96},{1,33},{33,65},{65,97},{2,34},{34,66},{66,9... | collective-permute-start | bytes 1572872 | tf_op jit(solution)/shard_map/ppermute | solution.py:20
  373.1 26.0 %collective-permute-start.5 = (bf16[8,4,32,256]{3,2,1,0:T(8,128)(2,1)S(1)}, bf16[8,4,32,256]{3,2,1,0:T(8,128)(2,1)S(1)}, u32[]{:S(2)}, u32[]{:S(2)}) collective-permute-start(bf16[8,4,32,256]{3,2,1,0:T(8,128)(2,1)S(1)} %get-tuple-element.14), channel_id=1, source_target_pairs={{32,0},{64,32},{96,64},{33,1},{65,33},{97,65},{34,2},{66,34},{98,6... | collective-permute-start | bytes 1572872 | tf_op jit(solution)/shard_map/ppermute | solution.py:21
  399.7 14.9 %collective-permute-start.6 = (bf16[8,40,4,256]{3,2,1,0:T(4,128)(2,1)S(1)}, bf16[8,40,4,256]{3,2,1,0:T(4,128)(2,1)S(1)}, u32[]{:S(2)}, u32[]{:S(2)}) collective-permute-start(bf16[8,40,4,256]{3,2,1,0:T(4,128)(2,1)S(1)} %get-tuple-element.8), channel_id=1, source_target_pairs={{0,1},{1,2},{2,3},{3,4},{4,5},{5,6},{6,7},{7,8},{8,9},{9,10},{10,1... | collective-permute-start | bytes 1966088 | tf_op jit(solution)/shard_map/ppermute | solution.py:20
  399.8 14.8 %collective-permute-start.7 = (bf16[8,40,4,256]{3,2,1,0:T(4,128)(2,1)S(1)}, bf16[8,40,4,256]{3,2,1,0:T(4,128)(2,1)S(1)}, u32[]{:S(2)}, u32[]{:S(2)}) collective-permute-start(bf16[8,40,4,256]{3,2,1,0:T(4,128)(2,1)S(1)} %get-tuple-element.7), channel_id=1, source_target_pairs={{1,0},{2,1},{3,2},{4,3},{5,4},{6,5},{7,6},{8,7},{9,8},{10,9},{11,1... | collective-permute-start | bytes 1966088 | tf_op jit(solution)/shard_map/ppermute | solution.py:21
  419.1 13.8 %copy-start.1 = (bf16[8,40,36,256]{3,2,1,0:T(8,128)(2,1)}, bf16[8,40,36,256]{3,2,1,0:T(8,128)(2,1)S(1)}, u32[]{:S(2)}) copy-start(bf16[8,40,36,256]{3,2,1,0:T(8,128)(2,1)S(1)} %get-tuple-element.5) | copy-start | bytes 17694724
where the time goes:
time: 476 us; the launch traced here: 469 us
  blocking collectives  257 us (54%)
  matrix products  126 us (26%)
  other arithmetic  37.6 us (8%)
  starting transfers between devices  23.9 us (5%)
  waiting for transfers between devices  22.4 us (5%)
    psum x2, blocking collectives, statistics(): lax.psum(group_total(jnp.sum(masked, axis=(1, 2))), ('lat', 'lon'))  131 us
    dot_general x18, matrix products, apply_kernel(): jnp.einsum('bijc,cd->bijd', shifted, weight[row_tap, col_tap], preferred_...  126 us
    psum x2, blocking collectives, statistics(): lax.psum(group_total(jnp.sum(squares, axis=(1, 2))), ('lat', 'lon'))  125 us
    ppermute x4, waiting for transfers between devices, extended(): after = lax.ppermute(leading, axis, down)  22.4 us
    ppermute x4, starting transfers between devices, extended(): after = lax.ppermute(leading, axis, down)  14.9 us
    concatenate x4, other arithmetic, extended(): array = jnp.concatenate([before, array, after], axis=dim)  13 us
  transfers between devices with their start and end apart: 8, of which 2 were waited for; matrix products, arithmetic and copies ran while one was open for 6% of the time, Pallas kernels for 0%

commit v1 on v0

--- a/solution.py
+++ b/solution.py
@@ -2,6 +2,7 @@
 import jax.numpy as jnp
 from jax import lax
 from jax.sharding import PartitionSpec as P
+from jax.lax import psum
 
 GROUPS = 32
 FIRST_DILATION = 2
@@ -54,7 +55,7 @@
     def group_total(chan_sums):
         return chan_sums.reshape(samples, GROUPS, group_size).sum(axis=2)
 
-    group_means = lax.psum(group_total(jnp.sum(masked, axis=(1, 2))), ("lat", "lon")) / live_count
+    group_means = psum(psum(group_total(jnp.sum(masked, axis=(1, 2))), "lat"), "lon") / live_count
     shifted = values_in - jnp.repeat(group_means, group_size, axis=1)[:, None, None, :]
     squares = shifted * shifted * live_mask[None, :, :, None]
     group_vars = lax.psum(group_total(jnp.sum(squares, axis=(1, 2))), ("lat", "lon")) / live_count

time: 476 us -> 525 us (1.10)
  blocking collectives: 257 us -> 304 us
    psum x2, blocking collectives: 125 us -> 157 us  [statistics(): lax.psum(group_total(jnp.sum(squares, axis=(1, 2))), ('lat', 'lon'))]
    psum x2 -> x4, blocking collectives: 131 us -> 148 us  [the longest x2 132 us: statistics(): psum(psum(group_total(jnp.sum(masked, axis=(1, 2))), 'lat'), 'lon')]
  transfers between devices with their start and end apart: 8 -> 8, of which waited for: 2 -> 2; matrix products, arithmetic and copies ran while one was open for 6% -> 5% of each run, Pallas kernels for 0% -> 0%
where the time goes in v1:
time: 525 us; the launch traced here: 518 us
  blocking collectives  304 us (58%)
  matrix products  126 us (24%)
  other arithmetic  37.6 us (7%)
  starting transfers between devices  25 us (5%)
  waiting for transfers between devices  22.4 us (4%)
    psum x2, blocking collectives, statistics(): lax.psum(group_total(jnp.sum(squares, axis=(1, 2))), ('lat', 'lon'))  157 us
    psum x2, blocking collectives, statistics(): psum(psum(group_total(jnp.sum(masked, axis=(1, 2))), 'lat'), 'lon')  132 us
    dot_general x18, matrix products, apply_kernel(): jnp.einsum('bijc,cd->bijd', shifted, weight[row_tap, col_tap], preferred_...  126 us
    ppermute x4, waiting for transfers between devices, extended(): after = lax.ppermute(leading, axis, down)  22.4 us
    ppermute x4, starting transfers between devices, extended(): after = lax.ppermute(leading, axis, down)  15.8 us
    psum x2, blocking collectives, statistics(): psum(group_total(jnp.sum(masked, axis=(1, 2))), 'lat')  15.6 us
    concatenate x4, other arithmetic, extended(): array = jnp.concatenate([before, array, after], axis=dim)  13 us
  transfers between devices with their start and end apart: 8, of which 2 were waited for; matrix products, arithmetic and copies ran while one was open for 5% of the time, Pallas kernels for 0%

profile of v1, /device:TPU:1, one launch (start us, length us, event | category | flops | bytes accessed | tf_op | source)
XLA Modules:
  0.0 517.9 jit_solution(14304971302876323023)
XLA Ops:
  4.2 8.8 %psum.42 = f32[8,32]{1,0:T(8,128)S(1)} all-reduce(f32[8,32]{1,0:T(8,128)S(1)} %reduce_sum.92), channel_id=1, replica_groups=mesh['lat'=4,'lon'=32] {'lat'}, use_global_device_ids=true, to_apply=%region_3.4 | all-reduce | flops 256 | bytes 2048 | tf_op jit(solution)/shard_map/psum | solution.py:58
  13.0 68.4 %psum.43 = f32[8,32]{1,0:T(8,128)S(1)} all-reduce(f32[8,32]{1,0:T(8,128)S(1)} %psum.42), channel_id=1, replica_groups=mesh['lat'=4,'lon'=32] {'lon'}, use_global_device_ids=true, to_apply=%region_4.5 | all-reduce | flops 256 | bytes 2048 | tf_op jit(solution)/shard_map/psum | solution.py:58
  87.5 79.0 %psum.44 = f32[8,32]{1,0:T(8,128)S(1)} all-reduce(f32[8,32]{1,0:T(8,128)S(1)} %reduce_sum.95), channel_id=1, replica_groups=mesh['lat'=4,'lon'=32] {'lat','lon'}, use_global_device_ids=true, to_apply=%region_8.9 | all-reduce | flops 256 | bytes 2048 | tf_op jit(solution)/shard_map/psum | solution.py:61
  166.8 4.3 fusion.12
  177.2 4.5 fusion.84
  185.0 6.1 %collective-permute-start.3 = (bf16[8,36,2,256]{3,2,1,0:T(2,128)(2,1)S(1)}, bf16[8,36,2,256]{3,2,1,0:T(2,128)(2,1)S(1)}, u32[]{:S(2)}, u32[]{:S(2)}) collective-permute-start(bf16[8,36,2,256]{3,2,1,0:T(2,128)(2,1)S(1)} %get-tuple-element.11), channel_id=1, source_target_pairs={{1,0},{2,1},{3,2},{4,3},{5,4},{6,5},{7,6},{8,7},{9,8},{10,9},{11,1... | collective-permute-start | bytes 884744 | tf_op jit(solution)/shard_map/ppermute | solution.py:22
  191.1 4.4 fusion.34
  195.5 4.5 fusion.38
  200.0 7.4 %pad_maximum_fusion.1 = (bf16[8,36,34,256]{3,2,1,0:T(8,128)(2,1)S(1)}, bf16[8,36,34,256]{3,2,1,0:T(8,128)(2,1)S(1)}) fusion(bf16[8,36,2,256]{3,2,1,0:T(2,128)(2,1)S(1)} %collective-permute-done.3, bf16[8,2,32,256]{3,2,1,0:T(8,128)(2,1)S(1)} %collective-permute-done.1, bf16[8,32,32,256]{3,2,1,0:T(8,128)(2,1)S(1)} %fusion.12, ...), kind=kLoop, calls=%fused_computation.35 | loop fusion | flops 40108032 | bytes 15335424 | tf_op jit(solution)/shard_map/concatenate | solution.py:23
  207.5 4.9 fusion.56
  212.4 4.4 fusion.60
  216.8 4.5 fusion.58
  221.3 4.5 fusion.62
  225.8 4.5 fusion.64
  230.2 26.7 %fusion.23 = bf16[8,32,32,256]{3,2,1,0:T(8,128)(2,1)} fusion(bf16[8,32,32,256]{3,2,1,0:T(8,128)(2,1)} %param.5, f32[8,32,32,256]{3,2,1,0:T(8,128)} %fusion.38, f32[8,32,32,256]{3,2,1,0:T(8,128)} %fusion.56, f32[8,32,32,256]{3,2,1,0:T(8,128)} %fusion.58, f32[8,32,32,256]{3,2,1,0:T(8,128)} %fusion.84, f32[8,32,32,256]{3,2,1,0:T(8,128)} %fusion.60, ...), kind=kOutput, calls=%fused_computation.29 | convolution fusion | flops 1098907648 | bytes 79823360 | tf_op jit(solution)/shard_map/bijc,cd->bijd/dot_general | solution.py:85
  260.3 6.8 %psum.45 = f32[8,32]{1,0:T(8,128)S(1)} all-reduce(f32[8,32]{1,0:T(8,128)S(1)} %reduce_sum.97), channel_id=1, replica_groups=mesh['lat'=4,'lon'=32] {'lat'}, use_global_device_ids=true, to_apply=%region_11.12 | all-reduce | flops 256 | bytes 2048 | tf_op jit(solution)/shard_map/psum | solution.py:58
  267.1 64.0 %psum.46 = f32[8,32]{1,0:T(8,128)S(1)} all-reduce(f32[8,32]{1,0:T(8,128)S(1)} %psum.45), channel_id=1, replica_groups=mesh['lat'=4,'lon'=32] {'lon'}, use_global_device_ids=true, to_apply=%region_12.13 | all-reduce | flops 256 | bytes 2048 | tf_op jit(solution)/shard_map/psum | solution.py:58
  335.1 77.5 %psum.47 = f32[8,32]{1,0:T(8,128)S(1)} all-reduce(f32[8,32]{1,0:T(8,128)S(1)} %reduce_sum.99), channel_id=1, replica_groups=mesh['lat'=4,'lon'=32] {'lat','lon'}, use_global_device_ids=true, to_apply=%region_15.16 | all-reduce | flops 256 | bytes 2048 | tf_op jit(solution)/shard_map/psum | solution.py:61
  412.8 4.3 fusion.17
  417.2 5.0 collective-permute-start.4
  424.1 4.5 fusion.74
  428.6 19.6 %collective-permute-done.5 = bf16[8,4,32,256]{3,2,1,0:T(8,128)(2,1)S(1)} collective-permute-done((bf16[8,4,32,256]{3,2,1,0:T(8,128)(2,1)S(1)}, bf16[8,4,32,256]{3,2,1,0:T(8,128)(2,1)S(1)}, u32[]{:S(2)}, u32[]{:S(2)}) %collective-permute-start.5) | collective-permute-done | bytes 524320 | tf_op jit(solution)/shard_map/ppermute | solution.py:22
  448.9 5.9 %collective-permute-start.7 = (bf16[8,40,4,256]{3,2,1,0:T(4,128)(2,1)S(1)}, bf16[8,40,4,256]{3,2,1,0:T(4,128)(2,1)S(1)}, u32[]{:S(2)}, u32[]{:S(2)}) collective-permute-start(bf16[8,40,4,256]{3,2,1,0:T(4,128)(2,1)S(1)} %get-tuple-element.7), channel_id=1, source_target_pairs={{1,0},{2,1},{3,2},{4,3},{5,4},{6,5},{7,6},{8,7},{9,8},{10,9},{11,1... | collective-permute-start | bytes 1966088 | tf_op jit(solution)/shard_map/ppermute | solution.py:22
  454.8 4.5 fusion.26
  459.2 4.5 fusion.30
  463.7 4.5 pad_maximum_fusion
  468.2 4.9 fusion.44
  473.1 4.5 fusion.48
  477.5 4.5 fusion.46
  482.1 4.5 fusion.50
  486.5 4.5 fusion.52
  491.0 26.7 %fusion.25 = bf16[8,32,32,256]{3,2,1,0:T(8,128)(2,1)} fusion(bf16[8,32,32,256]{3,2,1,0:T(8,128)(2,1)} %fusion.23, f32[8,32,32,256]{3,2,1,0:T(8,128)} %fusion.30, f32[8,32,32,256]{3,2,1,0:T(8,128)} %fusion.44, f32[8,32,32,256]{3,2,1,0:T(8,128)} %fusion.46, f32[8,32,32,256]{3,2,1,0:T(8,128)} %fusion.74, f32[8,32,32,256]{3,2,1,0:T(8,128)} %fusion.48, ...), kind=kOutput, calls=%fused_computation.31 | convolution fusion | flops 1098907648 | bytes 79823360 | tf_op jit(solution)/shard_map/bijc,cd->bijd/dot_general | solution.py:85
  (56 shorter events, 29.4 us)
Async XLA Ops:
  83.6 93.6 %copy-start.2 = (bf16[3,3,256,256]{3,2,1,0:T(8,128)(2,1)S(1)}, bf16[3,3,256,256]{3,2,1,0:T(8,128)(2,1)}, u32[]{:S(2)}) copy-start(bf16[3,3,256,256]{3,2,1,0:T(8,128)(2,1)} %param.8) | copy-start | bytes 3538948
  171.1 10.5 %collective-permute-start = (bf16[8,2,32,256]{3,2,1,0:T(8,128)(2,1)S(1)}, bf16[8,2,32,256]{3,2,1,0:T(8,128)(2,1)S(1)}, u32[]{:S(2)}, u32[]{:S(2)}) collective-permute-start(bf16[8,2,32,256]{3,2,1,0:T(8,128)(2,1)S(1)} %get-tuple-element.15), channel_id=1, source_target_pairs={{0,32},{32,64},{64,96},{1,33},{33,65},{65,97},{2,34},{34,66},{66,9... | collective-permute-start | bytes 786440 | tf_op jit(solution)/shard_map/ppermute | solution.py:21
  175.2 6.4 %copy-start.4 = (s32[8,2]{0,1:T(2,128)S(1)}, s32[8,2]{0,1:T(2,128)}, u32[]{:S(2)}) copy-start(s32[8,2]{0,1:T(2,128)} %param.7) | copy-start | bytes 196
  175.2 9.2 %collective-permute-start.1 = (bf16[8,2,32,256]{3,2,1,0:T(8,128)(2,1)S(1)}, bf16[8,2,32,256]{3,2,1,0:T(8,128)(2,1)S(1)}, u32[]{:S(2)}, u32[]{:S(2)}) collective-permute-start(bf16[8,2,32,256]{3,2,1,0:T(8,128)(2,1)S(1)} %get-tuple-element.16), channel_id=1, source_target_pairs={{32,0},{64,32},{96,64},{33,1},{65,33},{97,65},{34,2},{66,34},{98,6... | collective-permute-start | bytes 786440 | tf_op jit(solution)/shard_map/ppermute | solution.py:22
  184.9 15.1 %collective-permute-start.2 = (bf16[8,36,2,256]{3,2,1,0:T(2,128)(2,1)S(1)}, bf16[8,36,2,256]{3,2,1,0:T(2,128)(2,1)S(1)}, u32[]{:S(2)}, u32[]{:S(2)}) collective-permute-start(bf16[8,36,2,256]{3,2,1,0:T(2,128)(2,1)S(1)} %get-tuple-element.12), channel_id=1, source_target_pairs={{0,1},{1,2},{2,3},{3,4},{4,5},{5,6},{6,7},{7,8},{8,9},{9,10},{10,1... | collective-permute-start | bytes 884744 | tf_op jit(solution)/shard_map/ppermute | solution.py:21
  185.0 15.0 %collective-permute-start.3 = (bf16[8,36,2,256]{3,2,1,0:T(2,128)(2,1)S(1)}, bf16[8,36,2,256]{3,2,1,0:T(2,128)(2,1)S(1)}, u32[]{:S(2)}, u32[]{:S(2)}) collective-permute-start(bf16[8,36,2,256]{3,2,1,0:T(2,128)(2,1)S(1)} %get-tuple-element.11), channel_id=1, source_target_pairs={{1,0},{2,1},{3,2},{4,3},{5,4},{6,5},{7,6},{8,7},{9,8},{10,9},{11,1... | collective-permute-start | bytes 884744 | tf_op jit(solution)/shard_map/ppermute | solution.py:22
  207.5 13.8 %copy-start = (bf16[8,36,34,256]{3,2,1,0:T(8,128)(2,1)}, bf16[8,36,34,256]{3,2,1,0:T(8,128)(2,1)S(1)}, u32[]{:S(2)}) copy-start(bf16[8,36,34,256]{3,2,1,0:T(8,128)(2,1)S(1)} %get-tuple-element.9) | copy-start | bytes 15040516
  334.9 89.2 %copy-start.3 = (bf16[3,3,256,256]{3,2,1,0:T(8,128)(2,1)S(1)}, bf16[3,3,256,256]{3,2,1,0:T(8,128)(2,1)}, u32[]{:S(2)}) copy-start(bf16[3,3,256,256]{3,2,1,0:T(8,128)(2,1)} %param.9) | copy-start | bytes 3538948
  417.2 11.4 %collective-permute-start.4 = (bf16[8,4,32,256]{3,2,1,0:T(8,128)(2,1)S(1)}, bf16[8,4,32,256]{3,2,1,0:T(8,128)(2,1)S(1)}, u32[]{:S(2)}, u32[]{:S(2)}) collective-permute-start(bf16[8,4,32,256]{3,2,1,0:T(8,128)(2,1)S(1)} %get-tuple-element.13), channel_id=1, source_target_pairs={{0,32},{32,64},{64,96},{1,33},{33,65},{65,97},{2,34},{34,66},{66,9... | collective-permute-start | bytes 1572872 | tf_op jit(solution)/shard_map/ppermute | solution.py:21
  422.2 26.0 %collective-permute-start.5 = (bf16[8,4,32,256]{3,2,1,0:T(8,128)(2,1)S(1)}, bf16[8,4,32,256]{3,2,1,0:T(8,128)(2,1)S(1)}, u32[]{:S(2)}, u32[]{:S(2)}) collective-permute-start(bf16[8,4,32,256]{3,2,1,0:T(8,128)(2,1)S(1)} %get-tuple-element.14), channel_id=1, source_target_pairs={{32,0},{64,32},{96,64},{33,1},{65,33},{97,65},{34,2},{66,34},{98,6... | collective-permute-start | bytes 1572872 | tf_op jit(solution)/shard_map/ppermute | solution.py:22
  448.8 14.9 %collective-permute-start.6 = (bf16[8,40,4,256]{3,2,1,0:T(4,128)(2,1)S(1)}, bf16[8,40,4,256]{3,2,1,0:T(4,128)(2,1)S(1)}, u32[]{:S(2)}, u32[]{:S(2)}) collective-permute-start(bf16[8,40,4,256]{3,2,1,0:T(4,128)(2,1)S(1)} %get-tuple-element.8), channel_id=1, source_target_pairs={{0,1},{1,2},{2,3},{3,4},{4,5},{5,6},{6,7},{7,8},{8,9},{9,10},{10,1... | collective-permute-start | bytes 1966088 | tf_op jit(solution)/shard_map/ppermute | solution.py:21
  448.9 14.8 %collective-permute-start.7 = (bf16[8,40,4,256]{3,2,1,0:T(4,128)(2,1)S(1)}, bf16[8,40,4,256]{3,2,1,0:T(4,128)(2,1)S(1)}, u32[]{:S(2)}, u32[]{:S(2)}) collective-permute-start(bf16[8,40,4,256]{3,2,1,0:T(4,128)(2,1)S(1)} %get-tuple-element.7), channel_id=1, source_target_pairs={{1,0},{2,1},{3,2},{4,3},{5,4},{6,5},{7,6},{8,7},{9,8},{10,9},{11,1... | collective-permute-start | bytes 1966088 | tf_op jit(solution)/shard_map/ppermute | solution.py:22
  468.2 13.8 %copy-start.1 = (bf16[8,40,36,256]{3,2,1,0:T(8,128)(2,1)}, bf16[8,40,36,256]{3,2,1,0:T(8,128)(2,1)S(1)}, u32[]{:S(2)}) copy-start(bf16[8,40,36,256]{3,2,1,0:T(8,128)(2,1)S(1)} %get-tuple-element.5) | copy-start | bytes 17694724
